TPU v7x, 128 devices: a whole 4x4x4 slice. The times are simulated.
128 devices in a mesh: row: 16 (over z_lo, y, core), col: 8 (over x, z_hi).
Axes of the slice: x: 4, y: 4, z: 4 (z_hi: 2, z_lo: 2; z = z_hi * 2 + z_lo), core: 2. Of those that a mesh axis runs over, the one named last changes fastest.
Arguments:
- features: bfloat16 [32768, 128], P(('col', 'row')), may hold values from -6 to 6
- weight: bfloat16 [128, 256], replicated, may hold values from -0.5 to 0.5
- adj_values: bfloat16 [12288, 256, 256], P(('row', 'col')), may hold values from -0.0390625 to 0.0390625
- slot_rows: int32 [12288], P(('row', 'col')), may hold values from 0 to 7, as said below
- slot_cols: int32 [12288], P(('row', 'col')), may hold values from 0 to 15
- slot_live: int32 [128], P(('row', 'col')), may hold values from 13 to 96, as said below
- cotangent: bfloat16 [32768, 256], P(('row', 'col')), may hold values from -6 to 6
Outputs:
- output: bfloat16 [32768, 256], P(('row', 'col'))
- grad_features: bfloat16 [32768, 128], P(('col', 'row'))
- grad_weight: float32 [128, 256], replicated
Inputs may be any that keep to these rules, and one draw needn't show every extreme that they name: Within one device's slots the pairs (slot_rows, slot_cols) are distinct. `slot_live`: some device has all 96 slots live.
All inputs are finite; a program needn't handle non-finite values.
Results may differ from a plain program's by a relative error of at most 0.006.
Values may be sent and summed in bfloat16 or wider, within the bound.
A program may use at most 128 MiB of HBM per device.

v0:
```python
import math
import jax
import jax.numpy as jnp
from jax import lax
from jax.sharding import PartitionSpec as P


def silu_slope(value):
    sig = jax.nn.sigmoid(value)
    return sig * (1.0 + value * (1.0 - sig))


def block_product(adj_values, index_in, index_out, keep, source, count_out, transposed):
    slots, size = (adj_values.shape[0], adj_values.shape[1])
    width = source.shape[2]
    group = math.gcd(slots, 32)
    groups = slots // group

    def step(total, item):
        values, taken, placed, weights = item
        picked = source[taken]
        if transposed:
            product = jnp.einsum("sab,saf->sbf", values, picked, preferred_element_type=jnp.float32)
        else:
            product = jnp.einsum("sab,sbf->saf", values, picked, preferred_element_type=jnp.float32)
        return (total.at[placed].add(product * weights[:, None, None]), None)

    items = (
        adj_values.reshape(groups, group, size, size),
        index_in.reshape(groups, group),
        index_out.reshape(groups, group),
        keep.reshape(groups, group),
    )
    total, _ = lax.scan(step, jnp.zeros((count_out, size, width), jnp.float32), items)
    return total.reshape(count_out * size, width)


def body(features, weight, adj_values, slot_rows, slot_cols, slot_live, cotangent):
    size = adj_values.shape[1]
    slots = adj_values.shape[0]
    width = weight.shape[1]
    own_rows = features.shape[0]
    per_device = own_rows // size
    tile_rows = per_device * lax.axis_size("col")
    tile_cols = per_device * lax.axis_size("row")
    nodes = own_rows * lax.axis_size("row") * lax.axis_size("col")
    keep = (jnp.arange(slots, dtype=jnp.int32) < slot_live[0]).astype(jnp.float32)
    projected = jnp.dot(features, weight, preferred_element_type=jnp.float32).astype(jnp.bfloat16)
    column_rows = lax.all_gather(projected, "row", axis=0, tiled=True)
    column_blocks = column_rows.reshape(tile_cols, size, width)
    partial_value = block_product(
        adj_values, slot_cols, slot_rows, keep, column_blocks, tile_rows, False
    )
    summed = lax.psum_scatter(partial_value, "col", scatter_dimension=0, tiled=True)
    output = jax.nn.silu(summed).astype(jnp.bfloat16)
    grad_summed = (cotangent.astype(jnp.float32) * silu_slope(summed)).astype(jnp.bfloat16)
    grad_range = lax.all_gather(grad_summed, "col", axis=0, tiled=True)
    grad_blocks = grad_range.reshape(tile_rows, size, width)
    back = block_product(adj_values, slot_rows, slot_cols, keep, grad_blocks, tile_cols, True)
    grad_projected = lax.psum_scatter(back, "row", scatter_dimension=0, tiled=True).astype(
        jnp.bfloat16
    )
    grad_features = jnp.dot(grad_projected, weight.T, preferred_element_type=jnp.float32).astype(
        jnp.bfloat16
    )
    local_term = lax.dot_general(
        features, grad_projected, (((0,), (0,)), ((), ())), preferred_element_type=jnp.float32
    )
    grad_weight = lax.psum(local_term, ("row", "col")) / math.sqrt(nodes)
    return (output, grad_features, grad_weight)


def solution(mesh):
    placed = (
        P(("col", "row"), None),
        P(),
        P(("row", "col"), None, None),
        P(("row", "col")),
        P(("row", "col")),
        P(("row", "col")),
        P(("row", "col"), None),
    )
    return jax.shard_map(
        body,
        mesh=mesh,
        in_specs=placed,
        out_specs=(P(("row", "col"), None), P(("col", "row"), None), P()),
        check_vma=False,
    )
```

profile of v0, /device:TPU:1, one launch (start us, length us, event | category | flops | bytes accessed | tf_op | source)
XLA Modules:
  0.0 557.0 jit_solution(4911130216952027264)
XLA Ops:
  7.2 0.0 copy-start
  7.2 0.0 all-gather.3.cloned.1.call-start
  7.2 0.8 copy-done
  8.0 1.7 convolution_convert_fusion
  9.7 0.0 all-gather.3.cloned.1.call-update
  9.7 0.0 reduce-scatter.3.cloned.1.call-start
  10.4 0.7 reshape.149
  11.1 0.7 reshape.151
  11.9 35.7 %all-gather.3.cloned.1.call-done = bf16[4096,256]{1,0:T(8,128)(2,1)} async-done(((bf16[256,256]{1,0:T(8,128)(2,1)}), bf16[4096,256]{1,0:T(8,128)(2,1)}) %all-gather.3.cloned.1.call-update) | async-done | bytes 2097168 | tf_op jit(solution)/shard_map/all_gather | solution.py:49
  47.6 0.2 broadcast_in_dim.4
  47.8 0.0 copy-start.4
  47.8 72.4 %while.20 = (s32[]{:T(128)}, f32[8,256,256]{2,1,0:T(8,128)S(1)}, s32[3,32]{1,0:T(4,128)S(1)}, bf16[3,32,256,256]{3,2,1,0:T(8,128)(2,1)}, s32[3,32]{1,0:T(4,128)S...) while((s32[]{:T(128)}, f32[8,256,256]{2,1,0:T(8,128)S(1)}, s32[3,32]{1,0:T(4,128)S(1)}, ...), condition=%wide.region_2.3_spmd, body=%wide.region_0.2_spmd.sunk | while | flops 1077937408 | bytes 50337628 | solution.py:34
  47.8 4.4 gather_fusion
  52.2 7.9 %broadcast_multiply_fusion.5 = f32[32,256,256]{2,1,0:T(8,128)} fusion(f32[32]{0:T(128)S(1)} %fusion.42, bf16[32,256,256]{2,1,0:T(8,128)(2,1)} %gather_fusion, bf16[3,32,256,256]{3,2,1,0:T(8,128)(2,1)} %get-tuple-element.236, s32[]{:T(128)} %get-tuple-element.225), kind=kOutput, calls=%fused_computation.6.clone.1 | convolution fusion | flops 1075838976 | bytes 16777856 | tf_op jit(solution)/shard_map/while/body/eval_jaxpr/sab,sbf->saf/dot_general | solution.py:25
  60.2 11.8 %scatter_fusion = f32[8,256,256]{2,1,0:T(8,128)S(1)} fusion(f32[8,256,256]{2,1,0:T(8,128)S(1)} %get-tuple-element.226, s32[32]{0:T(128)S(1)} %get-tuple-element.206, f32[32,256,256]{2,1,0:T(8,128)} %broadcast_multiply_fusion.5), kind=kCustom, calls=%fused_computation.2.clone.1 | custom fusion | flops 2097152 | bytes 25165952 | tf_op jit(solution)/shard_map/while/body/eval_jaxpr/scatter-add | solution.py:26
  72.0 4.4 gather_fusion
  76.4 7.9 %broadcast_multiply_fusion.5 = f32[32,256,256]{2,1,0:T(8,128)} fusion(f32[32]{0:T(128)S(1)} %fusion.42, bf16[32,256,256]{2,1,0:T(8,128)(2,1)} %gather_fusion, bf16[3,32,256,256]{3,2,1,0:T(8,128)(2,1)} %get-tuple-element.236, s32[]{:T(128)} %get-tuple-element.225), kind=kOutput, calls=%fused_computation.6.clone.1 | convolution fusion | flops 1075838976 | bytes 16777856 | tf_op jit(solution)/shard_map/while/body/eval_jaxpr/sab,sbf->saf/dot_general | solution.py:25
  84.3 11.7 %scatter_fusion = f32[8,256,256]{2,1,0:T(8,128)S(1)} fusion(f32[8,256,256]{2,1,0:T(8,128)S(1)} %get-tuple-element.226, s32[32]{0:T(128)S(1)} %get-tuple-element.206, f32[32,256,256]{2,1,0:T(8,128)} %broadcast_multiply_fusion.5), kind=kCustom, calls=%fused_computation.2.clone.1 | custom fusion | flops 2097152 | bytes 25165952 | tf_op jit(solution)/shard_map/while/body/eval_jaxpr/scatter-add | solution.py:26
  96.1 4.4 gather_fusion
  100.5 7.9 %broadcast_multiply_fusion.5 = f32[32,256,256]{2,1,0:T(8,128)} fusion(f32[32]{0:T(128)S(1)} %fusion.42, bf16[32,256,256]{2,1,0:T(8,128)(2,1)} %gather_fusion, bf16[3,32,256,256]{3,2,1,0:T(8,128)(2,1)} %get-tuple-element.236, s32[]{:T(128)} %get-tuple-element.225), kind=kOutput, calls=%fused_computation.6.clone.1 | convolution fusion | flops 1075838976 | bytes 16777856 | tf_op jit(solution)/shard_map/while/body/eval_jaxpr/sab,sbf->saf/dot_general | solution.py:25
  108.4 11.7 %scatter_fusion = f32[8,256,256]{2,1,0:T(8,128)S(1)} fusion(f32[8,256,256]{2,1,0:T(8,128)S(1)} %get-tuple-element.226, s32[32]{0:T(128)S(1)} %get-tuple-element.206, f32[32,256,256]{2,1,0:T(8,128)} %broadcast_multiply_fusion.5), kind=kCustom, calls=%fused_computation.2.clone.1 | custom fusion | flops 2097152 | bytes 25165952 | tf_op jit(solution)/shard_map/while/body/eval_jaxpr/scatter-add | solution.py:26
  120.2 0.0 copy-start.1
  120.2 1.3 copy-done.1
  121.5 0.0 reduce-scatter.3.cloned.1.call-update
  121.6 0.0 all-gather.5.cloned.1.call-start
  121.6 75.0 %reduce-scatter.3.cloned.1.call-done = f32[256,256]{1,0:T(8,128)} async-done(((f32[2048,256]{1,0:T(8,128)}), f32[256,256]{1,0:T(8,128)}) %reduce-scatter.3.cloned.1.call-update) | async-done | bytes 262160 | tf_op jit(solution)/shard_map/reduce_scatter | solution.py:54
  196.6 0.0 copy-done.4
  196.6 1.8 multiply_convert_fusion
  198.4 0.0 all-gather.5.cloned.1.call-update
  198.4 0.0 reduce-scatter.5.cloned.1.call-start
  198.5 16.6 %copy.10 = bf16[96,256,256]{1,2,0:T(8,128)(2,1)} copy(bf16[96,256,256]{2,1,0:T(8,128)(2,1)} %bitcast.87) | data formatting | bytes 25165824 | tf_op args[2]
  215.1 30.2 %all-gather.5.cloned.1.call-done = bf16[2048,256]{1,0:T(8,128)(2,1)} async-done(((bf16[256,256]{1,0:T(8,128)(2,1)}), bf16[2048,256]{1,0:T(8,128)(2,1)}) %all-gather.5.cloned.1.call-update) | async-done | bytes 1048592 | tf_op jit(solution)/shard_map/all_gather | solution.py:57
  245.3 0.0 copy-start.2
  245.3 2.4 broadcast_in_dim.8
  247.7 0.0 copy-done.2
  247.7 87.2 %while.21 = (s32[]{:T(128)}, f32[16,256,256]{2,1,0:T(8,128)}, s32[3,32]{1,0:T(4,128)S(1)}, bf16[3,32,256,256]{2,3,1,0:T(8,128)(2,1)}, s32[3,32]{1,0:T(4,128)S(1)...) while((s32[]{:T(128)}, f32[16,256,256]{2,1,0:T(8,128)}, s32[3,32]{1,0:T(4,128)S(1)}, ...), condition=%wide.region_6.7_spmd, body=%wide.region_4.6_spmd.sunk | while | flops 1077937408 | bytes 50337628 | solution.py:34
  247.7 2.8 gather_fusion.1
  250.5 7.9 %broadcast_multiply_fusion.6 = f32[32,256,256]{2,1,0:T(8,128)} fusion(f32[32]{0:T(128)S(1)} %fusion.46, bf16[32,256,256]{2,1,0:T(8,128)(2,1)} %gather_fusion.1, bf16[3,32,256,256]{2,3,1,0:T(8,128)(2,1)} %get-tuple-element.260, s32[]{:T(128)} %get-tuple-element.249), kind=kOutput, calls=%fused_computation.22.clone.1 | convolution fusion | flops 1075838976 | bytes 16777856 | tf_op jit(solution)/shard_map/while/body/eval_jaxpr/sab,saf->sbf/dot_general | solution.py:23
  258.4 18.5 %scatter_fusion.1 = f32[16,256,256]{2,1,0:T(8,128)} fusion(f32[16,256,256]{2,1,0:T(8,128)} %get-tuple-element.250, s32[32]{0:T(128)S(1)} %get-tuple-element.215, f32[32,256,256]{2,1,0:T(8,128)} %broadcast_multiply_fusion.6), kind=kCustom, calls=%fused_computation.3.clone.1 | custom fusion | flops 2097152 | bytes 25165952 | tf_op jit(solution)/shard_map/while/body/eval_jaxpr/scatter-add | solution.py:26
  277.0 2.8 gather_fusion.1
  279.8 7.9 %broadcast_multiply_fusion.6 = f32[32,256,256]{2,1,0:T(8,128)} fusion(f32[32]{0:T(128)S(1)} %fusion.46, bf16[32,256,256]{2,1,0:T(8,128)(2,1)} %gather_fusion.1, bf16[3,32,256,256]{2,3,1,0:T(8,128)(2,1)} %get-tuple-element.260, s32[]{:T(128)} %get-tuple-element.249), kind=kOutput, calls=%fused_computation.22.clone.1 | convolution fusion | flops 1075838976 | bytes 16777856 | tf_op jit(solution)/shard_map/while/body/eval_jaxpr/sab,saf->sbf/dot_general | solution.py:23
  287.7 18.3 %scatter_fusion.1 = f32[16,256,256]{2,1,0:T(8,128)} fusion(f32[16,256,256]{2,1,0:T(8,128)} %get-tuple-element.250, s32[32]{0:T(128)S(1)} %get-tuple-element.215, f32[32,256,256]{2,1,0:T(8,128)} %broadcast_multiply_fusion.6), kind=kCustom, calls=%fused_computation.3.clone.1 | custom fusion | flops 2097152 | bytes 25165952 | tf_op jit(solution)/shard_map/while/body/eval_jaxpr/scatter-add | solution.py:26
  306.0 2.8 gather_fusion.1
  308.8 7.9 %broadcast_multiply_fusion.6 = f32[32,256,256]{2,1,0:T(8,128)} fusion(f32[32]{0:T(128)S(1)} %fusion.46, bf16[32,256,256]{2,1,0:T(8,128)(2,1)} %gather_fusion.1, bf16[3,32,256,256]{2,3,1,0:T(8,128)(2,1)} %get-tuple-element.260, s32[]{:T(128)} %get-tuple-element.249), kind=kOutput, calls=%fused_computation.22.clone.1 | convolution fusion | flops 1075838976 | bytes 16777856 | tf_op jit(solution)/shard_map/while/body/eval_jaxpr/sab,saf->sbf/dot_general | solution.py:23
  316.7 18.2 %scatter_fusion.1 = f32[16,256,256]{2,1,0:T(8,128)} fusion(f32[16,256,256]{2,1,0:T(8,128)} %get-tuple-element.250, s32[32]{0:T(128)S(1)} %get-tuple-element.215, f32[32,256,256]{2,1,0:T(8,128)} %broadcast_multiply_fusion.6), kind=kCustom, calls=%fused_computation.3.clone.1 | custom fusion | flops 2097152 | bytes 25165952 | tf_op jit(solution)/shard_map/while/body/eval_jaxpr/scatter-add | solution.py:26
  334.9 0.0 copy-start.3
  334.9 0.0 reduce-scatter.5.cloned.1.call-update
  335.0 0.0 all-reduce.2.cloned.1.call-start
  335.0 64.2 %reduce-scatter.5.cloned.1.call-done = f32[256,256]{1,0:T(8,128)} async-done(((f32[4096,256]{1,0:T(8,128)}), f32[256,256]{1,0:T(8,128)}) %reduce-scatter.5.cloned.1.call-update) | async-done | bytes 262160 | tf_op jit(solution)/shard_map/reduce_scatter | solution.py:60
  399.2 1.8 convolution_bitcast_fusion
  401.1 0.0 all-reduce.2.cloned.1.call-update
  401.1 0.0 copy-done.3
  401.1 1.8 convolution_convert_fusion.1
  402.9 145.9 %all-reduce.2.cloned.1.call-done = f32[128,256]{0,1:T(8,128)} async-done(((f32[128,256]{0,1:T(8,128)}), f32[128,256]{0,1:T(8,128)}) %all-reduce.2.cloned.1.call-update) | async-done | bytes 131088 | tf_op jit(solution)/shard_map/psum | solution.py:69
  548.8 0.9 broadcast_multiply_fusion.2
  549.7 0.8 copy.12
  (19 shorter events, 0.1 us)
Async XLA Ops:
  7.2 0.8 copy-start
  7.2 40.4 %all-gather.3.cloned.1.call-start = ((), (), s32[]{:S(2)}) async-start(), calls=%async_computation.2 | async-start | bytes 2228224 | tf_op jit(solution)/shard_map/all_gather | solution.py:49
  9.7 186.9 %reduce-scatter.3.cloned.1.call-start = ((), (), s32[]{:S(2)}) async-start(), calls=%async_computation.3 | async-start | bytes 2359296 | tf_op jit(solution)/shard_map/reduce_scatter | solution.py:54
  47.8 148.9 %copy-start.4 = (bf16[256,256]{1,0:T(8,128)(2,1)S(1)}, bf16[256,256]{1,0:T(8,128)(2,1)}, u32[]{:S(2)}) copy-start(bf16[256,256]{1,0:T(8,128)(2,1)} %param.17) | copy-start | bytes 393220
  120.2 1.3 copy-start.1
  121.6 123.7 %all-gather.5.cloned.1.call-start = ((), (), s32[]{:S(2)}) async-start(), calls=%async_computation.4 | async-start | bytes 1179648 | tf_op jit(solution)/shard_map/all_gather | solution.py:57
  198.4 200.8 %reduce-scatter.5.cloned.1.call-start = ((), (), s32[]{:S(2)}) async-start(), calls=%async_computation.5 | async-start | bytes 4456448 | tf_op jit(solution)/shard_map/reduce_scatter | solution.py:60
  245.3 2.4 copy-start.2
  334.9 66.1 %copy-start.3 = (bf16[128,256]{1,0:T(8,128)(2,1)S(1)}, bf16[128,256]{1,0:T(8,128)(2,1)}, u32[]{:S(2)}) copy-start(bf16[128,256]{1,0:T(8,128)(2,1)} %param.12) | copy-start | bytes 196612
  335.0 213.8 %all-reduce.2.cloned.1.call-start = ((), (), s32[]{:S(2)}) async-start(), calls=%async_computation.6 | async-start | bytes 262144 | tf_op jit(solution)/shard_map/psum | solution.py:69
Sparse Core Ops, SparseCore 0:
  10.3 37.2 all-gather.2
  121.7 74.9 reduce-scatter.2
  199.6 45.6 all-gather.4
  335.1 64.0 reduce-scatter.4
  404.4 144.3 all-reduce.1
where the time goes:
time: 558 us; the launch traced here: 557 us
  waiting for transfers between devices  351 us (63%)
  other arithmetic  93.1 us (17%)
  matrix products  52.9 us (9%)
  local copies, waits for them, and re-layouts  45.1 us (8%)
  between operations  14.5 us (3%)
    psum x1, waiting for transfers between devices, body(): grad_weight = lax.psum(local_term, ('row', 'col')) / math.sqrt(nodes)  146 us
    scatter-add x6, other arithmetic, step(): return (total.at[placed].add(product * weights[:, None, None]), None)  90.3 us
    reduce_scatter x1, waiting for transfers between devices, body(): lax.psum_scatter(partial_value, 'col', scatter_dimension=0, tiled=True)  75 us
    reduce_scatter x1, waiting for transfers between devices, body(): lax.psum_scatter(back, 'row', scatter_dimension=0, tiled=True)  64.2 us
    all_gather x1, waiting for transfers between devices, body(): column_rows = lax.all_gather(projected, 'row', axis=0, tiled=True)  35.7 us
    all_gather x1, waiting for transfers between devices, body(): grad_range = lax.all_gather(grad_summed, 'col', axis=0, tiled=True)  30.2 us
    dot_general x3, matrix products, step(): jnp.einsum('sab,sbf->saf', values, picked, preferred_element_type=jnp.flo...  23.8 us
    dot_general x3, matrix products, step(): jnp.einsum('sab,saf->sbf', values, picked, preferred_element_type=jnp.flo...  23.8 us
  transfers between devices with their start and end apart: 5, of which 5 were waited for; matrix products, arithmetic and copies ran while one was open for 4% of the time, Pallas kernels for 0%

commit v1 on v0

--- a/solution.py
+++ b/solution.py
@@ -66,7 +66,7 @@
     local_term = lax.dot_general(
         features, grad_projected, (((0,), (0,)), ((), ())), preferred_element_type=jnp.float32
     )
-    grad_weight = lax.psum(local_term, ("row", "col")) / math.sqrt(nodes)
+    grad_weight = jnp.sum(lax.all_gather(local_term, ("row", "col")), axis=0) / math.sqrt(nodes)
     return (output, grad_features, grad_weight)
 
 

time: 558 us -> 739 us (1.32)
  waiting for transfers between devices: 351 us -> 511 us
  local copies, waits for them, and re-layouts: 45.1 us -> 59.2 us
  other arithmetic: 93.1 us -> 101 us
    all_gather x0 -> x1, waiting for transfers between devices: none -> 305 us  [body(): lax.all_gather(local_term, ('row', 'col'))]
    psum x1 -> x0, waiting for transfers between devices: 146 us -> none  [body(): grad_weight = lax.psum(local_term, ('row', 'col')) / math.sqrt(nodes)]
    unnamed x12 -> x13, local copies, waits for them, and re-layouts: 19.5 us -> 33.6 us
    reduce_sum x0 -> x1, other arithmetic: none -> 8.39 us  [body(): jnp.sum(lax.all_gather(local_term, ('row', 'col')), axis=0)]
  transfers between devices with their start and end apart: 5 -> 5, of which waited for: 5 -> 5; matrix products, arithmetic and copies ran while one was open for 4% -> 3% of each run, Pallas kernels for 0% -> 0%
where the time goes in v1:
time: 739 us; the launch traced here: 738 us
  waiting for transfers between devices  511 us (69%)
  other arithmetic  101 us (14%)
  local copies, waits for them, and re-layouts  59.2 us (8%)
  matrix products  52.9 us (7%)
  between operations  14.5 us (2%)
    all_gather x1, waiting for transfers between devices, body(): lax.all_gather(local_term, ('row', 'col'))  305 us
    scatter-add x6, other arithmetic, step(): return (total.at[placed].add(product * weights[:, None, None]), None)  90.3 us
    reduce_scatter x1, waiting for transfers between devices, body(): lax.psum_scatter(partial_value, 'col', scatter_dimension=0, tiled=True)  75.1 us
    reduce_scatter x1, waiting for transfers between devices, body(): lax.psum_scatter(back, 'row', scatter_dimension=0, tiled=True)  64.2 us
    all_gather x1, waiting for transfers between devices, body(): column_rows = lax.all_gather(projected, 'row', axis=0, tiled=True)  35.7 us
    unnamed x13, local copies, waits for them, and re-layouts  33.6 us
    all_gather x1, waiting for transfers between devices, body(): grad_range = lax.all_gather(grad_summed, 'col', axis=0, tiled=True)  30.1 us
    dot_general x3, matrix products, step(): jnp.einsum('sab,sbf->saf', values, picked, preferred_element_type=jnp.flo...  23.8 us
  transfers between devices with their start and end apart: 5, of which 5 were waited for; matrix products, arithmetic and copies ran while one was open for 3% of the time, Pallas kernels for 0%

profile of v1, /device:TPU:1, one launch (start us, length us, event | category | flops | bytes accessed | tf_op | source)
XLA Modules:
  0.0 738.0 jit_solution(4248810342634226336)
XLA Ops:
  7.2 0.0 copy-start
  7.2 0.0 all-gather.5.cloned.1.call-start
  7.2 0.8 copy-done
  8.0 1.7 convolution_convert_fusion
  9.7 0.0 all-gather.5.cloned.1.call-update
  9.7 0.0 reduce-scatter.3.cloned.1.call-start
  10.4 0.7 reshape.149
  11.1 0.7 reshape.151
  11.9 35.7 %all-gather.5.cloned.1.call-done = bf16[4096,256]{1,0:T(8,128)(2,1)} async-done(((bf16[256,256]{1,0:T(8,128)(2,1)}), bf16[4096,256]{1,0:T(8,128)(2,1)}) %all-gather.5.cloned.1.call-update) | async-done | bytes 2097168 | tf_op jit(solution)/shard_map/all_gather | solution.py:49
  47.6 0.2 broadcast_in_dim.4
  47.8 0.0 copy-start.4
  47.8 72.4 %while.20 = (s32[]{:T(128)}, f32[8,256,256]{2,1,0:T(8,128)S(1)}, s32[3,32]{1,0:T(4,128)S(1)}, bf16[3,32,256,256]{3,2,1,0:T(8,128)(2,1)}, s32[3,32]{1,0:T(4,128)S...) while((s32[]{:T(128)}, f32[8,256,256]{2,1,0:T(8,128)S(1)}, s32[3,32]{1,0:T(4,128)S(1)}, ...), condition=%wide.region_2.3_spmd, body=%wide.region_0.2_spmd.sunk | while | flops 1077937408 | bytes 50337128 | solution.py:34
  47.8 4.4 gather_fusion
  52.2 7.9 %broadcast_multiply_fusion.5 = f32[32,256,256]{2,1,0:T(8,128)} fusion(f32[32]{0:T(128)S(1)} %fusion.42, bf16[32,256,256]{2,1,0:T(8,128)(2,1)} %gather_fusion, bf16[3,32,256,256]{3,2,1,0:T(8,128)(2,1)} %get-tuple-element.243, s32[]{:T(128)S(6)} %copy.21), kind=kOutput, calls=%fused_computation.6.clone.1 | convolution fusion | flops 1075838976 | bytes 16777348 | tf_op jit(solution)/shard_map/while/body/eval_jaxpr/sab,sbf->saf/dot_general | solution.py:25
  60.2 11.8 %scatter_fusion = f32[8,256,256]{2,1,0:T(8,128)S(1)} fusion(f32[8,256,256]{2,1,0:T(8,128)S(1)} %get-tuple-element.233, s32[32]{0:T(128)S(1)} %get-tuple-element.213, f32[32,256,256]{2,1,0:T(8,128)} %broadcast_multiply_fusion.5), kind=kCustom, calls=%fused_computation.2.clone.1 | custom fusion | flops 2097152 | bytes 25165952 | tf_op jit(solution)/shard_map/while/body/eval_jaxpr/scatter-add | solution.py:26
  72.0 4.4 gather_fusion
  76.4 7.9 %broadcast_multiply_fusion.5 = f32[32,256,256]{2,1,0:T(8,128)} fusion(f32[32]{0:T(128)S(1)} %fusion.42, bf16[32,256,256]{2,1,0:T(8,128)(2,1)} %gather_fusion, bf16[3,32,256,256]{3,2,1,0:T(8,128)(2,1)} %get-tuple-element.243, s32[]{:T(128)S(6)} %copy.21), kind=kOutput, calls=%fused_computation.6.clone.1 | convolution fusion | flops 1075838976 | bytes 16777348 | tf_op jit(solution)/shard_map/while/body/eval_jaxpr/sab,sbf->saf/dot_general | solution.py:25
  84.3 11.7 %scatter_fusion = f32[8,256,256]{2,1,0:T(8,128)S(1)} fusion(f32[8,256,256]{2,1,0:T(8,128)S(1)} %get-tuple-element.233, s32[32]{0:T(128)S(1)} %get-tuple-element.213, f32[32,256,256]{2,1,0:T(8,128)} %broadcast_multiply_fusion.5), kind=kCustom, calls=%fused_computation.2.clone.1 | custom fusion | flops 2097152 | bytes 25165952 | tf_op jit(solution)/shard_map/while/body/eval_jaxpr/scatter-add | solution.py:26
  96.1 4.4 gather_fusion
  100.5 7.9 %broadcast_multiply_fusion.5 = f32[32,256,256]{2,1,0:T(8,128)} fusion(f32[32]{0:T(128)S(1)} %fusion.42, bf16[32,256,256]{2,1,0:T(8,128)(2,1)} %gather_fusion, bf16[3,32,256,256]{3,2,1,0:T(8,128)(2,1)} %get-tuple-element.243, s32[]{:T(128)S(6)} %copy.21), kind=kOutput, calls=%fused_computation.6.clone.1 | convolution fusion | flops 1075838976 | bytes 16777348 | tf_op jit(solution)/shard_map/while/body/eval_jaxpr/sab,sbf->saf/dot_general | solution.py:25
  108.5 11.7 %scatter_fusion = f32[8,256,256]{2,1,0:T(8,128)S(1)} fusion(f32[8,256,256]{2,1,0:T(8,128)S(1)} %get-tuple-element.233, s32[32]{0:T(128)S(1)} %get-tuple-element.213, f32[32,256,256]{2,1,0:T(8,128)} %broadcast_multiply_fusion.5), kind=kCustom, calls=%fused_computation.2.clone.1 | custom fusion | flops 2097152 | bytes 25165952 | tf_op jit(solution)/shard_map/while/body/eval_jaxpr/scatter-add | solution.py:26
  120.2 0.0 copy-start.1
  120.2 1.3 copy-done.1
  121.6 0.0 reduce-scatter.3.cloned.1.call-update
  121.6 0.0 all-gather.7.cloned.1.call-start
  121.6 75.1 %reduce-scatter.3.cloned.1.call-done = f32[256,256]{1,0:T(8,128)} async-done(((f32[2048,256]{1,0:T(8,128)}), f32[256,256]{1,0:T(8,128)}) %reduce-scatter.3.cloned.1.call-update) | async-done | bytes 262160 | tf_op jit(solution)/shard_map/reduce_scatter | solution.py:54
  196.7 0.0 copy-done.4
  196.7 1.8 multiply_convert_fusion
  198.5 0.0 all-gather.7.cloned.1.call-update
  198.5 0.0 reduce-scatter.5.cloned.1.call-start
  198.6 16.6 %copy.12 = bf16[96,256,256]{1,2,0:T(8,128)(2,1)} copy(bf16[96,256,256]{2,1,0:T(8,128)(2,1)} %bitcast.92) | data formatting | bytes 25165824 | tf_op args[2]
  215.2 30.1 %all-gather.7.cloned.1.call-done = bf16[2048,256]{1,0:T(8,128)(2,1)} async-done(((bf16[256,256]{1,0:T(8,128)(2,1)}), bf16[2048,256]{1,0:T(8,128)(2,1)}) %all-gather.7.cloned.1.call-update) | async-done | bytes 1048592 | tf_op jit(solution)/shard_map/all_gather | solution.py:57
  245.3 0.0 copy-start.2
  245.3 2.4 broadcast_in_dim.8
  247.7 0.0 copy-done.2
  247.7 87.3 %while.21 = (s32[]{:T(128)}, f32[16,256,256]{2,1,0:T(8,128)}, s32[3,32]{1,0:T(4,128)S(1)}, bf16[3,32,256,256]{2,3,1,0:T(8,128)(2,1)}, s32[3,32]{1,0:T(4,128)S(1)...) while((s32[]{:T(128)}, f32[16,256,256]{2,1,0:T(8,128)}, s32[3,32]{1,0:T(4,128)S(1)}, ...), condition=%wide.region_6.7_spmd, body=%wide.region_4.6_spmd.sunk | while | flops 1077937408 | bytes 50337128 | solution.py:34
  247.8 2.8 gather_fusion.1
  250.5 7.9 %broadcast_multiply_fusion.6 = f32[32,256,256]{2,1,0:T(8,128)} fusion(f32[32]{0:T(128)S(1)} %fusion.46, bf16[32,256,256]{2,1,0:T(8,128)(2,1)} %gather_fusion.1, bf16[3,32,256,256]{2,3,1,0:T(8,128)(2,1)} %get-tuple-element.267, s32[]{:T(128)S(6)} %copy.27), kind=kOutput, calls=%fused_computation.22.clone.1 | convolution fusion | flops 1075838976 | bytes 16777348 | tf_op jit(solution)/shard_map/while/body/eval_jaxpr/sab,saf->sbf/dot_general | solution.py:23
  258.5 18.5 %scatter_fusion.1 = f32[16,256,256]{2,1,0:T(8,128)} fusion(f32[16,256,256]{2,1,0:T(8,128)} %get-tuple-element.257, s32[32]{0:T(128)S(1)} %get-tuple-element.222, f32[32,256,256]{2,1,0:T(8,128)} %broadcast_multiply_fusion.6), kind=kCustom, calls=%fused_computation.3.clone.1 | custom fusion | flops 2097152 | bytes 25165952 | tf_op jit(solution)/shard_map/while/body/eval_jaxpr/scatter-add | solution.py:26
  277.0 2.8 gather_fusion.1
  279.8 7.9 %broadcast_multiply_fusion.6 = f32[32,256,256]{2,1,0:T(8,128)} fusion(f32[32]{0:T(128)S(1)} %fusion.46, bf16[32,256,256]{2,1,0:T(8,128)(2,1)} %gather_fusion.1, bf16[3,32,256,256]{2,3,1,0:T(8,128)(2,1)} %get-tuple-element.267, s32[]{:T(128)S(6)} %copy.27), kind=kOutput, calls=%fused_computation.22.clone.1 | convolution fusion | flops 1075838976 | bytes 16777348 | tf_op jit(solution)/shard_map/while/body/eval_jaxpr/sab,saf->sbf/dot_general | solution.py:23
  287.7 18.3 %scatter_fusion.1 = f32[16,256,256]{2,1,0:T(8,128)} fusion(f32[16,256,256]{2,1,0:T(8,128)} %get-tuple-element.257, s32[32]{0:T(128)S(1)} %get-tuple-element.222, f32[32,256,256]{2,1,0:T(8,128)} %broadcast_multiply_fusion.6), kind=kCustom, calls=%fused_computation.3.clone.1 | custom fusion | flops 2097152 | bytes 25165952 | tf_op jit(solution)/shard_map/while/body/eval_jaxpr/scatter-add | solution.py:26
  306.1 2.8 gather_fusion.1
  308.8 7.9 %broadcast_multiply_fusion.6 = f32[32,256,256]{2,1,0:T(8,128)} fusion(f32[32]{0:T(128)S(1)} %fusion.46, bf16[32,256,256]{2,1,0:T(8,128)(2,1)} %gather_fusion.1, bf16[3,32,256,256]{2,3,1,0:T(8,128)(2,1)} %get-tuple-element.267, s32[]{:T(128)S(6)} %copy.27), kind=kOutput, calls=%fused_computation.22.clone.1 | convolution fusion | flops 1075838976 | bytes 16777348 | tf_op jit(solution)/shard_map/while/body/eval_jaxpr/sab,saf->sbf/dot_general | solution.py:23
  316.8 18.2 %scatter_fusion.1 = f32[16,256,256]{2,1,0:T(8,128)} fusion(f32[16,256,256]{2,1,0:T(8,128)} %get-tuple-element.257, s32[32]{0:T(128)S(1)} %get-tuple-element.222, f32[32,256,256]{2,1,0:T(8,128)} %broadcast_multiply_fusion.6), kind=kCustom, calls=%fused_computation.3.clone.1 | custom fusion | flops 2097152 | bytes 25165952 | tf_op jit(solution)/shard_map/while/body/eval_jaxpr/scatter-add | solution.py:26
  335.0 0.0 copy-start.3
  335.0 0.0 reduce-scatter.5.cloned.1.call-update
  335.0 0.0 all-gather.9.cloned.1.call-start
  335.1 64.2 %reduce-scatter.5.cloned.1.call-done = f32[256,256]{1,0:T(8,128)} async-done(((f32[4096,256]{1,0:T(8,128)}), f32[256,256]{1,0:T(8,128)}) %reduce-scatter.5.cloned.1.call-update) | async-done | bytes 262160 | tf_op jit(solution)/shard_map/reduce_scatter | solution.py:60
  399.3 1.8 convolution_bitcast_fusion
  401.1 0.0 all-gather.9.cloned.1.call-update
  401.1 0.0 copy-done.3
  401.1 1.8 convolution_convert_fusion.1
  402.9 305.3 %all-gather.9.cloned.1.call-done = f32[16384,256]{0,1:T(8,128)} async-done(((f32[128,256]{0,1:T(8,128)}), f32[16384,256]{0,1:T(8,128)}) %all-gather.9.cloned.1.call-update) | async-done | bytes 16777232 | tf_op jit(solution)/shard_map/all_gather | solution.py:69
  708.2 14.1 %copy.16 = f32[32,8,128,128]{3,2,1,0:T(8,128)} copy(f32[32,8,128,128]{3,1,2,0:T(8,128)} %bitcast.94) | data formatting | bytes 33554432
  722.3 8.4 %bitcast_reduce_fusion = f32[128,256]{0,1:T(8,128)S(1)} fusion(f32[32,8,128,128]{3,2,1,0:T(8,128)} %copy.16), kind=kLoop, calls=%fused_computation.36 | loop fusion | flops 4161536 | bytes 16908288 | tf_op jit(solution)/shard_map/reduce_sum | solution.py:69
  730.7 0.8 copy.14
  (20 shorter events, 0.2 us)
Async XLA Ops:
  7.2 0.8 copy-start
  7.2 40.4 %all-gather.5.cloned.1.call-start = ((), (), s32[]{:S(2)}) async-start(), calls=%async_computation.2 | async-start | bytes 2228224 | tf_op jit(solution)/shard_map/all_gather | solution.py:49
  9.7 187.0 %reduce-scatter.3.cloned.1.call-start = ((), (), s32[]{:S(2)}) async-start(), calls=%async_computation.3 | async-start | bytes 2359296 | tf_op jit(solution)/shard_map/reduce_scatter | solution.py:54
  47.8 149.0 %copy-start.4 = (bf16[256,256]{1,0:T(8,128)(2,1)S(1)}, bf16[256,256]{1,0:T(8,128)(2,1)}, u32[]{:S(2)}) copy-start(bf16[256,256]{1,0:T(8,128)(2,1)} %param.17) | copy-start | bytes 393220
  120.2 1.3 copy-start.1
  121.6 123.7 %all-gather.7.cloned.1.call-start = ((), (), s32[]{:S(2)}) async-start(), calls=%async_computation.4 | async-start | bytes 1179648 | tf_op jit(solution)/shard_map/all_gather | solution.py:57
  198.5 200.7 %reduce-scatter.5.cloned.1.call-start = ((), (), s32[]{:S(2)}) async-start(), calls=%async_computation.5 | async-start | bytes 4456448 | tf_op jit(solution)/shard_map/reduce_scatter | solution.py:60
  245.3 2.4 copy-start.2
  335.0 66.1 %copy-start.3 = (bf16[128,256]{1,0:T(8,128)(2,1)S(1)}, bf16[128,256]{1,0:T(8,128)(2,1)}, u32[]{:S(2)}) copy-start(bf16[128,256]{1,0:T(8,128)(2,1)} %param.12) | copy-start | bytes 196612
  335.0 373.2 %all-gather.9.cloned.1.call-start = ((), (), s32[]{:S(2)}) async-start(), calls=%async_computation.6 | async-start | bytes 16908288 | tf_op jit(solution)/shard_map/all_gather | solution.py:69
Sparse Core Ops, SparseCore 0:
  10.3 37.2 all-gather.4
  121.7 74.9 reduce-scatter.2
  199.6 45.6 all-gather.6
  335.1 64.0 reduce-scatter.4
  401.3 306.8 all-gather.8
